TPU v7x, 32 devices: a whole 2x2x4 slice. The times are simulated.
32 devices in a mesh: expert: 16 (over z, y, core), tensor: 2 (over x).
Axes of the slice: x: 2, y: 2, z: 4, core: 2. Of those that a mesh axis runs over, the one named last changes fastest.
Arguments:
- tokens: bfloat16 [4096, 2048], P(('expert', 'tensor')), may hold values from -6 to 6
- assignment: int32 [4096], P(('expert', 'tensor')), may hold values from 0 to 15, as said below
- norm_gain: float32 [2048], replicated, may hold values from 0.25 to 1.75
- centroids: bfloat16 [16, 2048], replicated, may hold values from -0.125 to 0.125
- w_in: bfloat16 [16, 2048, 8192], P('expert', None, 'tensor'), may hold values from -0.125 to 0.125
- w_out: bfloat16 [16, 8192, 2048], P('expert', 'tensor'), may hold values from -0.0625 to 0.0625
Outputs:
- mixed: bfloat16 [4096, 2048], P(('expert', 'tensor'))
Inputs may be any that keep to these rules, and one draw needn't show every extreme that they name: `assignment`: in each device's block of 128 consecutive tokens every expert is named exactly 8 times.
All inputs are finite; a program needn't handle non-finite values.
Results may differ from a plain program's by a relative error of at most 0.006.
Values may be sent and summed in bfloat16 or wider, within the bound.
A program may use at most 64 MiB of HBM per device.

v0:
```python
import jax
import jax.numpy as jnp
from jax import lax
from jax.sharding import PartitionSpec as P


def layer_norm(values, gain):
    widened = values.astype(jnp.float32)
    average = jnp.mean(widened, axis=1, keepdims=True)
    centred = widened - average
    variance = jnp.mean(centred * centred, axis=1, keepdims=True)
    return centred * lax.rsqrt(variance + 1e-05) * gain


def body(tokens, assignment, norm_gain, centroids, w_in, w_out):
    tok_rows = tokens.shape[0]
    num_experts = centroids.shape[0]
    per_expert = tok_rows // num_experts
    normed = layer_norm(tokens, norm_gain).astype(jnp.bfloat16)
    logits = jnp.dot(tokens, centroids.T, preferred_element_type=jnp.float32)
    column_ids = lax.broadcasted_iota(jnp.int32, (tok_rows, num_experts), 1)
    picked = jnp.sum(jnp.where(assignment[:, None] == column_ids, logits, 0.0), axis=1)
    gate_value = jax.nn.sigmoid(picked)
    same_expert = assignment[:, None] == assignment[None, :]
    row_ids = lax.broadcasted_iota(jnp.int32, (tok_rows, tok_rows), 0)
    col_ids = lax.broadcasted_iota(jnp.int32, (tok_rows, tok_rows), 1)
    rank_in = jnp.sum((same_expert & (col_ids < row_ids)).astype(jnp.int32), axis=1)
    slot_of = assignment * per_expert + rank_in
    ordering = jnp.argsort(slot_of)
    ordered_rows = normed[ordering]
    arrived = lax.all_to_all(ordered_rows, "expert", split_axis=0, concat_axis=0, tiled=True)
    w_first = w_in[0]
    w_second = w_out[0]
    hidden = jax.nn.gelu(
        jnp.dot(
            lax.all_gather(arrived, "tensor", axis=0, tiled=True),
            w_first,
            preferred_element_type=jnp.float32,
        ),
        approximate=True,
    ).astype(jnp.bfloat16)
    partials = jnp.dot(hidden, w_second, preferred_element_type=jnp.float32).astype(jnp.bfloat16)
    summed = (
        lax.psum_scatter(partials, "tensor", scatter_dimension=0, tiled=True)
        .astype(jnp.float32)
        .astype(jnp.bfloat16)
    )
    returned = lax.all_to_all(summed, "expert", split_axis=0, concat_axis=0, tiled=True)
    expert_out = returned[slot_of]
    mixed = tokens.astype(jnp.float32) + gate_value[:, None] * expert_out.astype(jnp.float32)
    return mixed.astype(jnp.bfloat16)


def solution(mesh):
    return jax.shard_map(
        body,
        mesh=mesh,
        in_specs=(
            P(("expert", "tensor"), None),
            P(("expert", "tensor")),
            P(),
            P(),
            P("expert", None, "tensor"),
            P("expert", "tensor", None),
        ),
        out_specs=P(("expert", "tensor"), None),
        check_vma=False,
    )
```

profile of v0, /device:TPU:0, one launch (start us, length us, event | category | flops | bytes accessed | tf_op | source)
XLA Modules:
  0.0 124.0 jit_solution(12280007484877348894)
XLA Ops:
  6.5 0.0 copy-start
  6.5 0.0 all-gather.2.cloned.1.call-start
  6.5 1.2 convert_reduce_fusion
  7.8 1.3 %fusion.27 = f32[128]{0:T(128)S(1)} fusion(bf16[128,2048]{1,0:T(8,128)(2,1)} %param.6, f32[128]{0:T(128)S(1)} %broadcast_multiply_fusion), kind=kLoop, calls=%fused_computation.26 | loop fusion | flops 1048448 | bytes 525312 | tf_op jit(solution)/shard_map/reduce_sum | solution.py:11
  9.1 0.9 convert_reduce_fusion.1
  10.0 0.7 compare_select_fusion
  10.7 2.5 %sort.17 = (s32[128]{0:T(128)}, s32[128]{0:T(128)S(1)}) sort(s32[128]{0:T(128)S(1)} %get-tuple-element.8, s32[128]{0:T(128)S(1)} %iota.22), dimensions={0}, to_apply=%region_4.5 | sort | flops 896 | bytes 2048 | tf_op jit(solution)/shard_map/jit(argsort)/sort | solution.py:29
  13.2 1.4 %fusion.29 = bf16[128,2048]{1,0:T(8,128)(2,1)S(1)} fusion(bf16[128,2048]{1,0:T(8,128)(2,1)} %param.6, f32[2048]{0:T(1024)} %param.8, f32[128]{0:T(128)S(1)} %add_rsqrt_fusion, f32[128]{0:T(128)S(1)} %broadcast_multiply_fusion), kind=kLoop, calls=%fused_computation.28 | loop fusion | flops 1310720 | bytes 1057792 | tf_op jit(solution)/shard_map/convert_element_type | solution.py:19
  14.7 0.9 gather_fusion
  15.6 21.6 %all_to_all.24 = bf16[16,8,2048]{2,1,0:T(8,128)(2,1)} all-to-all(bf16[16,8,2048]{2,1,0:T(8,128)(2,1)S(1)} %bitcast.22), channel_id=1, replica_groups=mesh['expert'=16,'tensor'=2] {'expert'}, dimensions={0} | all-to-all | bytes 1048576 | tf_op jit(solution)/shard_map/all_to_all | solution.py:31
  37.2 0.0 all-gather.2.cloned.1.call-update
  37.2 0.0 copy-start.1
  37.2 0.0 copy-start.2
  37.2 0.0 reduce-scatter.2.cloned.1.call-start
  37.3 20.9 %all-gather.2.cloned.1.call-done = bf16[256,2048]{1,0:T(8,128)(2,1)} async-done(((bf16[128,2048]{1,0:T(8,128)(2,1)}), bf16[256,2048]{1,0:T(8,128)(2,1)}) %all-gather.2.cloned.1.call-update) | async-done | bytes 1048592 | tf_op jit(solution)/shard_map/all_gather | solution.py:36
  58.2 16.6 %fusion.16 = bf16[256,2048]{1,0:T(8,128)(2,1)} fusion(bf16[1,4096,2048]{2,1,0:T(8,128)(2,1)} %param.11, bf16[256,2048]{1,0:T(8,128)(2,1)} %all-gather.2.cloned.1.call-done, bf16[1,2048,4096]{2,1,0:T(8,128)(2,1)} %param.10), kind=kOutput, calls=%fused_computation.15 | convolution fusion | flops 8599896064 | bytes 35651584 | tf_op jit(solution)/shard_map/dot_general | solution.py:42
  74.7 0.0 reduce-scatter.2.cloned.1.call-update
  74.7 20.5 %reduce-scatter.2.cloned.1.call-done = bf16[128,2048]{1,0:T(8,128)(2,1)} async-done(((bf16[256,2048]{1,0:T(8,128)(2,1)}), bf16[128,2048]{1,0:T(8,128)(2,1)}) %reduce-scatter.2.cloned.1.call-update) | async-done | bytes 524304 | tf_op jit(solution)/shard_map/reduce_scatter | solution.py:44
  95.3 5.6 %all-to-all-start.1 = ((bf16[16,8,2048]{2,1,0:T(8,128)(2,1)}), bf16[16,8,2048]{2,1,0:T(8,128)(2,1)S(1)}, u32[]{:S(2)}, u32[]{:S(2)}) async-start(bf16[16,8,2048]{2,1,0:T(8,128)(2,1)} %bitcast.24), calls=%async_computation.2 | async-start | bytes 1048576 | tf_op jit(solution)/shard_map/all_to_all | solution.py:48
  100.9 0.0 copy-done
  100.9 0.0 copy-done.1
  100.9 0.0 copy-done.2
  101.0 0.3 fusion.26
  101.2 14.0 %all-to-all-done.1 = bf16[16,8,2048]{2,1,0:T(8,128)(2,1)S(1)} async-done(((bf16[16,8,2048]{2,1,0:T(8,128)(2,1)}), bf16[16,8,2048]{2,1,0:T(8,128)(2,1)S(1)}, u32[]{:S(2)}, u32[]{:S(2)}) %all-to-all-start.1) | async-done | bytes 524320 | tf_op jit(solution)/shard_map/all_to_all | solution.py:48
  115.2 0.9 gather_fusion.1
  116.1 1.0 fusion.30
  (7 shorter events, 0.0 us)
Async XLA Ops:
  6.5 94.4 %copy-start = (bf16[16,2048]{1,0:T(8,128)(2,1)S(1)}, bf16[16,2048]{1,0:T(8,128)(2,1)}, u32[]{:S(2)}) copy-start(bf16[16,2048]{1,0:T(8,128)(2,1)} %param.9) | copy-start | bytes 196612
  6.5 51.6 %all-gather.2.cloned.1.call-start = ((), (), s32[]{:S(2)}) async-start(), calls=%async_computation.3 | async-start | bytes 1572864 | tf_op jit(solution)/shard_map/all_gather | solution.py:36
  37.2 63.7 %copy-start.1 = (bf16[128,2048]{1,0:T(8,128)(2,1)S(1)}, bf16[128,2048]{1,0:T(8,128)(2,1)}, u32[]{:S(2)}) copy-start(bf16[128,2048]{1,0:T(8,128)(2,1)} %param.6) | copy-start | bytes 1572868
  37.2 63.7 %copy-start.2 = (s32[128]{0:T(128)S(1)}, s32[128]{0:T(128)}, u32[]{:S(2)}) copy-start(s32[128]{0:T(128)} %param.7) | copy-start | bytes 1540
  37.2 58.0 %reduce-scatter.2.cloned.1.call-start = ((), (), s32[]{:S(2)}) async-start(), calls=%async_computation.4 | async-start | bytes 1572864 | tf_op jit(solution)/shard_map/reduce_scatter | solution.py:44
  95.3 19.9 %all-to-all-start.1 = ((bf16[16,8,2048]{2,1,0:T(8,128)(2,1)}), bf16[16,8,2048]{2,1,0:T(8,128)(2,1)S(1)}, u32[]{:S(2)}, u32[]{:S(2)}) async-start(bf16[16,8,2048]{2,1,0:T(8,128)(2,1)} %bitcast.24), calls=%async_computation.2 | async-start | bytes 1048576 | tf_op jit(solution)/shard_map/all_to_all | solution.py:48
Sparse Core Ops, SparseCore 0:
  37.3 20.7 all-gather.1
  74.9 20.3 reduce-scatter.1
where the time goes:
time: 124 us
  waiting for transfers between devices  55.4 us (45%)
  blocking collectives  21.6 us (17%)
  matrix products  16.8 us (14%)
  between operations  13.5 us (11%)
  other arithmetic  9.13 us (7%)
  starting transfers between devices  5.66 us (5%)
  local copies, waits for them, and re-layouts  1.89 us (2%)
    all_to_all x1, blocking collectives, body(): lax.all_to_all(ordered_rows, 'expert', split_axis=0, concat_axis=0, tiled...  21.6 us
    all_gather x1, waiting for transfers between devices, body(): lax.all_gather(arrived, 'tensor', axis=0, tiled=True)  20.9 us
    reduce_scatter x1, waiting for transfers between devices, body(): lax.psum_scatter(partials, 'tensor', scatter_dimension=0, tiled=True)  20.5 us
    dot_general x1, matrix products, body(): jnp.dot(hidden, w_second, preferred_element_type=jnp.float32)  16.6 us
    all_to_all x1, waiting for transfers between devices, body(): lax.all_to_all(summed, 'expert', split_axis=0, concat_axis=0, tiled=True)  14 us
    all_to_all x1, starting transfers between devices, body(): lax.all_to_all(summed, 'expert', split_axis=0, concat_axis=0, tiled=True)  5.62 us
    sort x1, other arithmetic, body(): ordering = jnp.argsort(slot_of)  2.54 us
  transfers between devices with their start and end apart: 3, of which 3 were waited for; matrix products, arithmetic and copies ran while one was open for 0% of the time, Pallas kernels for 0%

commit v1 on v0

v1 whole, which is shorter than its diff:
```python
import functools

import jax
import jax.numpy as jnp
from jax import lax
from jax.experimental import pallas as pl
from jax.experimental.pallas import tpu as pltpu
from jax.sharding import PartitionSpec as P

MESH = pl.DeviceIdType.MESH
F32 = jnp.float32
BF16 = jnp.bfloat16
CHUNKS = 8
TILE = 512
LAG = 3


def to_blocks(values, dims):
    return values.reshape(*dims, values.shape[-1]).astype(BF16)


def to_rows(blocks):
    wide = blocks.astype(F32)
    return wide.reshape(-1, wide.shape[-1]).astype(BF16)


def kernel(
    n_exp, n_ten, n_chunk,
    tok_ref, assign_ref, gain_ref, cent_ref, w_in_ref, w_out_ref,
    out_ref,
    w1, w2, send, gath, acc, hid, part, part_in, summed, ret,
    w1_sem, w2_sem, a_send, a_recv, g_send, g_recv, p_send, p_recv, r_send, r_recv,
):
    me = lax.axis_index("expert")
    mt = lax.axis_index("tensor")
    rows, width = tok_ref.shape
    per = rows // n_exp
    dc = width // n_chunk
    hidden = w1.shape[2]
    tile = min(TILE, hidden)

    barrier = pltpu.get_barrier_semaphore()

    @pl.loop(1, n_exp)
    def _(k):
        pl.semaphore_signal(barrier, inc=1, device_id={"expert": lax.rem(me + k, n_exp)}, device_id_type=MESH)

    for k in range(1, n_ten):
        pl.semaphore_signal(barrier, inc=1, device_id={"tensor": lax.rem(mt + k, n_ten)}, device_id_type=MESH)

    def w1_copy(c):
        return pltpu.make_async_copy(w_in_ref.at[0, pl.ds(c * dc, dc)], w1.at[c], w1_sem.at[c])

    def w2_copy(c):
        return pltpu.make_async_copy(w_out_ref.at[0, :, pl.ds(c * dc, dc)], w2.at[c], w2_sem.at[c])

    for c in range(n_chunk):
        w1_copy(c).start()
    for c in range(n_chunk):
        w2_copy(c).start()

    expert_of = assign_ref[...]
    onehot = lax.broadcasted_iota(jnp.int32, (n_exp, rows), 0) == expert_of
    row_id = lax.broadcasted_iota(jnp.int32, (rows, rows), 0)
    col_id = lax.broadcasted_iota(jnp.int32, (rows, rows), 1)
    before = jnp.where(row_id < col_id, 1.0, 0.0).astype(BF16)
    rank = jnp.dot(jnp.where(onehot, 1.0, 0.0).astype(BF16), before, preferred_element_type=F32)
    start = lax.broadcasted_iota(jnp.int32, (n_exp, rows), 0).astype(F32) * float(per)
    slot = jnp.sum(jnp.where(onehot, rank + start, 0.0), axis=0, keepdims=True)
    diagonal = row_id == col_id
    slot_col = jnp.sum(jnp.where(diagonal, slot, 0.0), axis=1, keepdims=True)
    perm = jnp.where(row_id.astype(F32) == slot, 1.0, 0.0).astype(BF16)
    back = jnp.where(col_id.astype(F32) == slot_col, 1.0, 0.0).astype(BF16)

    wide = tok_ref[...].astype(F32)
    average = jnp.mean(wide, axis=1, keepdims=True)
    centred = wide - average
    scale = lax.rsqrt(jnp.mean(centred * centred, axis=1, keepdims=True) + 1e-05)

    pl.semaphore_wait(barrier, n_exp - 1 + n_ten - 1)

    def spread(src, dst, c, sends, recvs, slot_ref):
        @pl.loop(1, n_exp)
        def _(k):
            peer = lax.rem(me + k, n_exp)
            pltpu.make_async_remote_copy(
                src_ref=src.at[c, peer], dst_ref=slot_ref(dst, c, me),
                send_sem=sends.at[c], recv_sem=recvs.at[c],
                device_id={"expert": peer}, device_id_type=MESH,
            ).start()

    def spread_all(src, dst, c, sends, recvs, slots_ref):
        return pltpu.make_async_remote_copy(
            src_ref=src.at[c, pl.ds(0, n_exp - 1)], dst_ref=slots_ref(dst, c),
            send_sem=sends.at[c], recv_sem=recvs.at[c],
            device_id={"expert": lax.rem(me + 1, n_exp)}, device_id_type=MESH,
        )

    gath_slot = lambda ref, c, i: ref.at[c, mt, i]
    gath_slots = lambda ref, c: ref.at[c, mt, pl.ds(0, n_exp - 1)]
    ret_slot = lambda ref, c, i: ref.at[c, i]
    ret_slots = lambda ref, c: ref.at[c, pl.ds(0, n_exp - 1)]

    for c in range(n_chunk):
        cols = slice(c * dc, (c + 1) * dc)
        normed = ((tok_ref[:, cols].astype(F32) - average) * scale * gain_ref[:, cols]).astype(BF16)
        ordered = jnp.dot(perm, normed, preferred_element_type=F32)
        send[c] = to_blocks(ordered, (n_exp, per))
        spread(send, gath, c, a_send, a_recv, gath_slot)
        gath[c, mt, me] = send[c, me]

    logits = lax.dot_general(cent_ref[...], tok_ref[...], (((1,), (1,)), ((), ())), preferred_element_type=F32)
    picked = jnp.sum(jnp.where(onehot, logits, 0.0), axis=0, keepdims=True)
    gate_row = jax.nn.sigmoid(picked)
    gate = jnp.sum(jnp.where(diagonal, gate_row, 0.0), axis=1, keepdims=True)

    def partner_copies(src, dst, c, sends, recvs, own):
        copies = []
        for k in range(1, n_ten):
            other = lax.rem(mt + k, n_ten)
            copies.append(pltpu.make_async_remote_copy(
                src_ref=src.at[c, mt if own else other], dst_ref=dst.at[c, mt],
                send_sem=sends.at[c, k - 1], recv_sem=recvs.at[c, k - 1],
                device_id={"tensor": other}, device_id_type=MESH,
            ))
        return copies

    def first(c):
        w1_copy(c).wait()
        for copy in partner_copies(gath, gath, c, g_send, g_recv, True):
            copy.wait_recv()
        x = to_rows(gath[c])
        last = c == n_chunk - 1

        @pl.loop(0, hidden // tile)
        def _(n):
            at = pl.ds(pl.multiple_of(n * tile, tile), tile)
            got = jnp.dot(x, w1[c, :, at], preferred_element_type=F32)
            if c > 0:
                got = got + acc[:, at]
            if last:
                hid[:, at] = jax.nn.gelu(got, approximate=True).astype(BF16)
            else:
                acc[:, at] = got

    for c in range(n_chunk):
        spread_all(send, gath, c, a_send, a_recv, gath_slots).wait_recv()
        for copy in partner_copies(gath, gath, c, g_send, g_recv, True):
            copy.start()
        if c > 0:
            first(c - 1)
    first(n_chunk - 1)

    def reduce(c):
        for copy in partner_copies(part, part_in, c, p_send, p_recv, False):
            copy.wait_recv()
        total = part[c, mt].astype(F32)
        for k in range(1, n_ten):
            total = total + part_in[c, lax.rem(mt + k, n_ten)].astype(F32)
        summed[c] = total.astype(BF16)
        spread(summed, ret, c, r_send, r_recv, ret_slot)
        ret[c, me] = summed[c, me]

    for c in range(n_chunk):
        w2_copy(c).wait()
        got = jnp.dot(hid[...], w2[c], preferred_element_type=F32)
        part[c] = to_blocks(got, (n_ten, n_exp, per))
        for copy in partner_copies(part, part_in, c, p_send, p_recv, False):
            copy.start()
        if c >= LAG:
            reduce(c - LAG)
    for c in range(n_chunk - LAG, n_chunk):
        reduce(c)

    for c in range(n_chunk):
        cols = slice(c * dc, (c + 1) * dc)
        spread_all(summed, ret, c, r_send, r_recv, ret_slots).wait_recv()
        expert_out = jnp.dot(back, to_rows(ret[c]), preferred_element_type=F32)
        out_ref[:, cols] = (tok_ref[:, cols].astype(F32) + gate * expert_out).astype(BF16)

    for c in range(n_chunk):
        spread_all(send, gath, c, a_send, a_recv, gath_slots).wait_send()
        spread_all(summed, ret, c, r_send, r_recv, ret_slots).wait_send()
        for copy in partner_copies(gath, gath, c, g_send, g_recv, True):
            copy.wait_send()
        for copy in partner_copies(part, part_in, c, p_send, p_recv, False):
            copy.wait_send()


def body(n_exp, n_ten, tokens, assignment, norm_gain, centroids, w_in, w_out):
    rows, width = tokens.shape
    per = rows // n_exp
    hidden = w_in.shape[2]
    n_chunk = CHUNKS
    dc = width // n_chunk
    vmem = pl.BlockSpec(memory_space=pltpu.VMEM)
    hbm = pl.BlockSpec(memory_space=pl.ANY)
    dma = pltpu.SemaphoreType.DMA
    return pl.pallas_call(
        functools.partial(kernel, n_exp, n_ten, n_chunk),
        out_shape=jax.ShapeDtypeStruct(tokens.shape, tokens.dtype),
        in_specs=[vmem, vmem, vmem, vmem, hbm, hbm],
        out_specs=vmem,
        scratch_shapes=[
            pltpu.VMEM((n_chunk, dc, hidden), BF16),
            pltpu.VMEM((n_chunk, hidden, dc), BF16),
            pltpu.VMEM((n_chunk, n_exp, per, dc), BF16),
            pltpu.VMEM((n_chunk, n_ten, n_exp, per, dc), BF16),
            pltpu.VMEM((n_ten * rows, hidden), F32),
            pltpu.VMEM((n_ten * rows, hidden), BF16),
            pltpu.VMEM((n_chunk, n_ten, n_exp, per, dc), BF16),
            pltpu.VMEM((n_chunk, n_ten, n_exp, per, dc), BF16),
            pltpu.VMEM((n_chunk, n_exp, per, dc), BF16),
            pltpu.VMEM((n_chunk, n_exp, per, dc), BF16),
            dma((n_chunk,)), dma((n_chunk,)),
            dma((n_chunk,)), dma((n_chunk,)),
            dma((n_chunk, n_ten - 1)), dma((n_chunk, n_ten - 1)),
            dma((n_chunk, n_ten - 1)), dma((n_chunk, n_ten - 1)),
            dma((n_chunk,)), dma((n_chunk,)),
        ],
        compiler_params=pltpu.CompilerParams(
            collective_id=0, has_side_effects=True, vmem_limit_bytes=64_000_000
        ),
    )(tokens, assignment.reshape(1, rows), norm_gain.reshape(1, width), centroids, w_in, w_out)


def solution(mesh):
    return jax.shard_map(
        functools.partial(body, mesh.shape["expert"], mesh.shape["tensor"]),
        mesh=mesh,
        in_specs=(
            P(("expert", "tensor"), None),
            P(("expert", "tensor")),
            P(),
            P(),
            P("expert", None, "tensor"),
            P("expert", "tensor", None),
        ),
        out_specs=P(("expert", "tensor"), None),
        check_vma=False,
    )
```

time: 124 us -> 58.8 us (0.47)
  Pallas kernels: 0 us -> 56.7 us
  waiting for transfers between devices: 55.4 us -> 0 us
  blocking collectives: 21.6 us -> 0 us
  matrix products: 16.8 us -> 0 us
  between operations: 13.5 us -> 0.01 us
  other arithmetic: 9.13 us -> 0 us
  starting transfers between devices: 5.66 us -> 0 us
    pallas_call x0 -> x1, Pallas kernels: none -> 56.7 us  [body(): pl.pallas_call(functools.partial(kernel, n_exp, n_ten, n_chunk), out_shap...]
    all_to_all x1 -> x0, blocking collectives: 21.6 us -> none  [body(): lax.all_to_all(ordered_rows, 'expert', split_axis=0, concat_axis=0, tiled...]
    all_gather x1 -> x0, waiting for transfers between devices: 20.9 us -> none  [body(): lax.all_gather(arrived, 'tensor', axis=0, tiled=True)]
    reduce_scatter x1 -> x0, waiting for transfers between devices: 20.5 us -> none  [body(): lax.psum_scatter(partials, 'tensor', scatter_dimension=0, tiled=True)]
    dot_general x2 -> x0, matrix products: 16.8 us -> none  [the longest x1 16.6 us: body(): jnp.dot(hidden, w_second, preferred_element_type=jnp.float32)]
    all_to_all x1 -> x0, waiting for transfers between devices: 14 us -> none  [body(): lax.all_to_all(summed, 'expert', split_axis=0, concat_axis=0, tiled=True)]
    all_to_all x1 -> x0, starting transfers between devices: 5.62 us -> none  [body(): lax.all_to_all(summed, 'expert', split_axis=0, concat_axis=0, tiled=True)]
    reduce_sum x3 -> x0, other arithmetic: 3.46 us -> none  [the longest x1 1.33 us: layer_norm(): variance = jnp.mean(centred * centred, axis=1, keepdims=True)]
  transfers between devices with their start and end apart: 3 -> 0, of which waited for: 3 -> 0; matrix products, arithmetic and copies ran while one was open for 0% -> 0% of each run, Pallas kernels for 0% -> 0%
where the time goes in v1:
time: 58.8 us; the launch traced here: 58.6 us
  Pallas kernels  56.7 us (96%)
  local copies, waits for them, and re-layouts  1.88 us (3%)
    pallas_call x1, Pallas kernels, body(): pl.pallas_call(functools.partial(kernel, n_exp, n_ten, n_chunk), out_shap...  56.7 us
    unnamed x1, local copies, waits for them, and re-layouts  1.88 us

profile of v1, /device:TPU:0, one launch (start us, length us, event | category | flops | bytes accessed | tf_op | source)
XLA Modules:
  0.0 58.6 jit_solution(8689471636596532882)
XLA Ops:
  0.0 56.7 %shard_map.64 = bf16[128,2048]{1,0:T(8,128)(2,1)} custom-call(bf16[128,2048]{1,0:T(8,128)(2,1)} %tok_ref.1, s32[1,128]{1,0:T(1,128)} %bitcast.3, f32[1,2048]{1,0:T(1,128)} %bitcast.2, bf16[16,2048]{1,0:T(8,128)(2,1)} %cent_ref.1, bf16[1,2048,4096]{2,1,0:T(8,128)(2,1)} %w_in_ref.1, bf16[1,4096,2048]{2,1,0:T(8,128)(2,1)} %w_out_ref.1), custom_call_target="tpu_custom_call" | custom-call | tf_op jit(solution)/shard_map/pallas_call | solution.py:199
  56.8 1.9 %copy.8 = bf16[128,2048]{1,0:T(8,128)(2,1)} copy(bf16[128,2048]{1,0:T(8,128)(2,1)} %shard_map.64) | data formatting | bytes 1048576

commit v2 on v1

--- a/solution.py
+++ b/solution.py
@@ -10,9 +10,9 @@
 MESH = pl.DeviceIdType.MESH
 F32 = jnp.float32
 BF16 = jnp.bfloat16
-CHUNKS = 8
+CHUNKS = 4
 TILE = 512
-LAG = 3
+LAG = 2
 
 
 def to_blocks(values, dims):
@@ -101,13 +101,16 @@
     ret_slot = lambda ref, c, i: ref.at[c, i]
     ret_slots = lambda ref, c: ref.at[c, pl.ds(0, n_exp - 1)]
 
-    for c in range(n_chunk):
+    def prepare(c):
         cols = slice(c * dc, (c + 1) * dc)
         normed = ((tok_ref[:, cols].astype(F32) - average) * scale * gain_ref[:, cols]).astype(BF16)
         ordered = jnp.dot(perm, normed, preferred_element_type=F32)
         send[c] = to_blocks(ordered, (n_exp, per))
         spread(send, gath, c, a_send, a_recv, gath_slot)
         gath[c, mt, me] = send[c, me]
+
+    for c in range(2):
+        prepare(c)
 
     logits = lax.dot_general(cent_ref[...], tok_ref[...], (((1,), (1,)), ((), ())), preferred_element_type=F32)
     picked = jnp.sum(jnp.where(onehot, logits, 0.0), axis=0, keepdims=True)
@@ -147,6 +150,8 @@
         spread_all(send, gath, c, a_send, a_recv, gath_slots).wait_recv()
         for copy in partner_copies(gath, gath, c, g_send, g_recv, True):
             copy.start()
+        if c + 2 < n_chunk:
+            prepare(c + 2)
         if c > 0:
             first(c - 1)
     first(n_chunk - 1)

time: 58.8 us -> 53.1 us (0.903)
  Pallas kernels: 56.7 us -> 51 us
    pallas_call x1, Pallas kernels: 56.7 us -> 51 us  [body(): pl.pallas_call(functools.partial(kernel, n_exp, n_ten, n_chunk), out_shap...]
where the time goes in v2:
time: 53.1 us; the launch traced here: 52.9 us
  Pallas kernels  51 us (96%)
  local copies, waits for them, and re-layouts  1.88 us (4%)
    pallas_call x1, Pallas kernels, body(): pl.pallas_call(functools.partial(kernel, n_exp, n_ten, n_chunk), out_shap...  51 us
    unnamed x1, local copies, waits for them, and re-layouts  1.88 us

profile of v2, /device:TPU:0, one launch (start us, length us, event | category | flops | bytes accessed | tf_op | source)
XLA Modules:
  0.0 52.9 jit_solution(17481182339646548253)
XLA Ops:
  0.0 51.0 %shard_map.64 = bf16[128,2048]{1,0:T(8,128)(2,1)} custom-call(bf16[128,2048]{1,0:T(8,128)(2,1)} %tok_ref.1, s32[1,128]{1,0:T(1,128)} %bitcast.3, f32[1,2048]{1,0:T(1,128)} %bitcast.2, bf16[16,2048]{1,0:T(8,128)(2,1)} %cent_ref.1, bf16[1,2048,4096]{2,1,0:T(8,128)(2,1)} %w_in_ref.1, bf16[1,4096,2048]{2,1,0:T(8,128)(2,1)} %w_out_ref.1), custom_call_target="tpu_custom_call" | custom-call | tf_op jit(solution)/shard_map/pallas_call | solution.py:204
  51.0 1.9 %copy.8 = bf16[128,2048]{1,0:T(8,128)(2,1)} copy(bf16[128,2048]{1,0:T(8,128)(2,1)} %shard_map.64) | data formatting | bytes 1048576

commit v3 on v2

--- a/solution.py
+++ b/solution.py
@@ -10,7 +10,7 @@
 MESH = pl.DeviceIdType.MESH
 F32 = jnp.float32
 BF16 = jnp.bfloat16
-CHUNKS = 4
+PARTS = (2, 2, 2, 2)
 TILE = 512
 LAG = 2
 
@@ -25,7 +25,7 @@
 
 
 def kernel(
-    n_exp, n_ten, n_chunk,
+    n_exp, n_ten,
     tok_ref, assign_ref, gain_ref, cent_ref, w_in_ref, w_out_ref,
     out_ref,
     w1, w2, send, gath, acc, hid, part, part_in, summed, ret,
@@ -35,9 +35,13 @@
     mt = lax.axis_index("tensor")
     rows, width = tok_ref.shape
     per = rows // n_exp
-    dc = width // n_chunk
-    hidden = w1.shape[2]
+    n_chunk = len(PARTS)
+    unit = width // sum(PARTS)
+    hidden = w1.shape[1]
     tile = min(TILE, hidden)
+
+    def span(c):
+        return pl.ds(sum(PARTS[:c]) * unit, PARTS[c] * unit)
 
     barrier = pltpu.get_barrier_semaphore()
 
@@ -49,10 +53,10 @@
         pl.semaphore_signal(barrier, inc=1, device_id={"tensor": lax.rem(mt + k, n_ten)}, device_id_type=MESH)
 
     def w1_copy(c):
-        return pltpu.make_async_copy(w_in_ref.at[0, pl.ds(c * dc, dc)], w1.at[c], w1_sem.at[c])
+        return pltpu.make_async_copy(w_in_ref.at[0, span(c)], w1.at[span(c)], w1_sem.at[c])
 
     def w2_copy(c):
-        return pltpu.make_async_copy(w_out_ref.at[0, :, pl.ds(c * dc, dc)], w2.at[c], w2_sem.at[c])
+        return pltpu.make_async_copy(w_out_ref.at[0, :, span(c)], w2.at[:, span(c)], w2_sem.at[c])
 
     for c in range(n_chunk):
         w1_copy(c).start()
@@ -80,34 +84,33 @@
     pl.semaphore_wait(barrier, n_exp - 1 + n_ten - 1)
 
     def spread(src, dst, c, sends, recvs, slot_ref):
-        @pl.loop(1, n_exp)
-        def _(k):
+        for k in sorted(range(1, n_exp), key=lambda k: abs(2 * k - n_exp)):
             peer = lax.rem(me + k, n_exp)
             pltpu.make_async_remote_copy(
-                src_ref=src.at[c, peer], dst_ref=slot_ref(dst, c, me),
+                src_ref=src.at[peer, :, span(c)], dst_ref=slot_ref(dst, c, me),
                 send_sem=sends.at[c], recv_sem=recvs.at[c],
                 device_id={"expert": peer}, device_id_type=MESH,
             ).start()
 
     def spread_all(src, dst, c, sends, recvs, slots_ref):
         return pltpu.make_async_remote_copy(
-            src_ref=src.at[c, pl.ds(0, n_exp - 1)], dst_ref=slots_ref(dst, c),
+            src_ref=src.at[pl.ds(0, n_exp - 1), :, span(c)], dst_ref=slots_ref(dst, c),
             send_sem=sends.at[c], recv_sem=recvs.at[c],
             device_id={"expert": lax.rem(me + 1, n_exp)}, device_id_type=MESH,
         )
 
-    gath_slot = lambda ref, c, i: ref.at[c, mt, i]
-    gath_slots = lambda ref, c: ref.at[c, mt, pl.ds(0, n_exp - 1)]
-    ret_slot = lambda ref, c, i: ref.at[c, i]
-    ret_slots = lambda ref, c: ref.at[c, pl.ds(0, n_exp - 1)]
+    gath_slot = lambda ref, c, i: ref.at[mt, i, :, span(c)]
+    gath_slots = lambda ref, c: ref.at[mt, pl.ds(0, n_exp - 1), :, span(c)]
+    ret_slot = lambda ref, c, i: ref.at[i, :, span(c)]
+    ret_slots = lambda ref, c: ref.at[pl.ds(0, n_exp - 1), :, span(c)]
 
     def prepare(c):
-        cols = slice(c * dc, (c + 1) * dc)
+        cols = span(c)
         normed = ((tok_ref[:, cols].astype(F32) - average) * scale * gain_ref[:, cols]).astype(BF16)
         ordered = jnp.dot(perm, normed, preferred_element_type=F32)
-        send[c] = to_blocks(ordered, (n_exp, per))
+        send[:, :, cols] = to_blocks(ordered, (n_exp, per))
         spread(send, gath, c, a_send, a_recv, gath_slot)
-        gath[c, mt, me] = send[c, me]
+        gath[mt, me, :, cols] = send[me, :, cols]
 
     for c in range(2):
         prepare(c)
@@ -122,7 +125,7 @@
         for k in range(1, n_ten):
             other = lax.rem(mt + k, n_ten)
             copies.append(pltpu.make_async_remote_copy(
-                src_ref=src.at[c, mt if own else other], dst_ref=dst.at[c, mt],
+                src_ref=src.at[mt if own else other, :, :, span(c)], dst_ref=dst.at[mt, :, :, span(c)],
                 send_sem=sends.at[c, k - 1], recv_sem=recvs.at[c, k - 1],
                 device_id={"tensor": other}, device_id_type=MESH,
             ))
@@ -132,13 +135,13 @@
         w1_copy(c).wait()
         for copy in partner_copies(gath, gath, c, g_send, g_recv, True):
             copy.wait_recv()
-        x = to_rows(gath[c])
+        x = to_rows(gath[:, :, :, span(c)])
         last = c == n_chunk - 1
 
         @pl.loop(0, hidden // tile)
         def _(n):
             at = pl.ds(pl.multiple_of(n * tile, tile), tile)
-            got = jnp.dot(x, w1[c, :, at], preferred_element_type=F32)
+            got = jnp.dot(x, w1[span(c), at], preferred_element_type=F32)
             if c > 0:
                 got = got + acc[:, at]
             if last:
@@ -159,17 +162,17 @@
     def reduce(c):
         for copy in partner_copies(part, part_in, c, p_send, p_recv, False):
             copy.wait_recv()
-        total = part[c, mt].astype(F32)
+        total = part[mt, :, :, span(c)].astype(F32)
         for k in range(1, n_ten):
-            total = total + part_in[c, lax.rem(mt + k, n_ten)].astype(F32)
-        summed[c] = total.astype(BF16)
+            total = total + part_in[lax.rem(mt + k, n_ten), :, :, span(c)].astype(F32)
+        summed[:, :, span(c)] = total.astype(BF16)
         spread(summed, ret, c, r_send, r_recv, ret_slot)
-        ret[c, me] = summed[c, me]
+        ret[me, :, span(c)] = summed[me, :, span(c)]
 
     for c in range(n_chunk):
         w2_copy(c).wait()
-        got = jnp.dot(hid[...], w2[c], preferred_element_type=F32)
-        part[c] = to_blocks(got, (n_ten, n_exp, per))
+        got = jnp.dot(hid[...], w2[:, span(c)], preferred_element_type=F32)
+        part[:, :, :, span(c)] = to_blocks(got, (n_ten, n_exp, per))
         for copy in partner_copies(part, part_in, c, p_send, p_recv, False):
             copy.start()
         if c >= LAG:
@@ -178,9 +181,9 @@
         reduce(c)
 
     for c in range(n_chunk):
-        cols = slice(c * dc, (c + 1) * dc)
+        cols = span(c)
         spread_all(summed, ret, c, r_send, r_recv, ret_slots).wait_recv()
-        expert_out = jnp.dot(back, to_rows(ret[c]), preferred_element_type=F32)
+        expert_out = jnp.dot(back, to_rows(ret[:, :, cols]), preferred_element_type=F32)
         out_ref[:, cols] = (tok_ref[:, cols].astype(F32) + gate * expert_out).astype(BF16)
 
     for c in range(n_chunk):
@@ -196,27 +199,26 @@
     rows, width = tokens.shape
     per = rows // n_exp
     hidden = w_in.shape[2]
-    n_chunk = CHUNKS
-    dc = width // n_chunk
+    n_chunk = len(PARTS)
     vmem = pl.BlockSpec(memory_space=pltpu.VMEM)
     hbm = pl.BlockSpec(memory_space=pl.ANY)
     dma = pltpu.SemaphoreType.DMA
     return pl.pallas_call(
-        functools.partial(kernel, n_exp, n_ten, n_chunk),
+        functools.partial(kernel, n_exp, n_ten),
         out_shape=jax.ShapeDtypeStruct(tokens.shape, tokens.dtype),
         in_specs=[vmem, vmem, vmem, vmem, hbm, hbm],
         out_specs=vmem,
         scratch_shapes=[
-            pltpu.VMEM((n_chunk, dc, hidden), BF16),
-            pltpu.VMEM((n_chunk, hidden, dc), BF16),
-            pltpu.VMEM((n_chunk, n_exp, per, dc), BF16),
-            pltpu.VMEM((n_chunk, n_ten, n_exp, per, dc), BF16),
+            pltpu.VMEM((width, hidden), BF16),
+            pltpu.VMEM((hidden, width), BF16),
+            pltpu.VMEM((n_exp, per, width), BF16),
+            pltpu.VMEM((n_ten, n_exp, per, width), BF16),
             pltpu.VMEM((n_ten * rows, hidden), F32),
             pltpu.VMEM((n_ten * rows, hidden), BF16),
-            pltpu.VMEM((n_chunk, n_ten, n_exp, per, dc), BF16),
-            pltpu.VMEM((n_chunk, n_ten, n_exp, per, dc), BF16),
-            pltpu.VMEM((n_chunk, n_exp, per, dc), BF16),
-            pltpu.VMEM((n_chunk, n_exp, per, dc), BF16),
+            pltpu.VMEM((n_ten, n_exp, per, width), BF16),
+            pltpu.VMEM((n_ten, n_exp, per, width), BF16),
+            pltpu.VMEM((n_exp, per, width), BF16),
+            pltpu.VMEM((n_exp, per, width), BF16),
             dma((n_chunk,)), dma((n_chunk,)),
             dma((n_chunk,)), dma((n_chunk,)),
             dma((n_chunk, n_ten - 1)), dma((n_chunk, n_ten - 1)),

time: 53.1 us -> 54.8 us (1.032)
  Pallas kernels: 51 us -> 52.7 us
    pallas_call x1, Pallas kernels: 51 us -> 52.7 us  [body(): pl.pallas_call(functools.partial(kernel, n_exp, n_ten), out_shape=jax.Sha...]
where the time goes in v3:
time: 54.8 us; the launch traced here: 54.6 us
  Pallas kernels  52.7 us (96%)
  local copies, waits for them, and re-layouts  1.88 us (3%)
    pallas_call x1, Pallas kernels, body(): pl.pallas_call(functools.partial(kernel, n_exp, n_ten), out_shape=jax.Sha...  52.7 us
    unnamed x1, local copies, waits for them, and re-layouts  1.88 us

profile of v3, /device:TPU:0, one launch (start us, length us, event | category | flops | bytes accessed | tf_op | source)
XLA Modules:
  0.0 54.6 jit_solution(2298884070710039341)
XLA Ops:
  0.0 52.7 %shard_map.64 = bf16[128,2048]{1,0:T(8,128)(2,1)} custom-call(bf16[128,2048]{1,0:T(8,128)(2,1)} %tok_ref.1, s32[1,128]{1,0:T(1,128)} %bitcast.3, f32[1,2048]{1,0:T(1,128)} %bitcast.2, bf16[16,2048]{1,0:T(8,128)(2,1)} %cent_ref.1, bf16[1,2048,4096]{2,1,0:T(8,128)(2,1)} %w_in_ref.1, bf16[1,4096,2048]{2,1,0:T(8,128)(2,1)} %w_out_ref.1), custom_call_target="tpu_custom_call" | custom-call | tf_op jit(solution)/shard_map/pallas_call | solution.py:206
  52.7 1.9 %copy.8 = bf16[128,2048]{1,0:T(8,128)(2,1)} copy(bf16[128,2048]{1,0:T(8,128)(2,1)} %shard_map.64) | data formatting | bytes 1048576
